TPU v7x, 32 devices: a whole 2x2x4 slice. The times are simulated.
32 devices in a mesh: grp: 2 (over x), seq: 8 (over z, y), mdl: 2 (over core).
Axes of the slice: x: 2, y: 2, z: 4, core: 2. Of those that a mesh axis runs over, the one named last changes fastest.
Arguments:
- signal: float32 [8, 128, 8192], P('grp', 'mdl', 'seq'), parts along dimension 0, may hold values from -6 to 6
- lengths: int32 [8], P('grp'), parts along dimension 0, may hold values from 1 to 64, 160 in all
- chan_weight: bfloat16 [128, 128, 16], P('mdl'), may hold values from -0.5 to 0.5
- up_weight: bfloat16 [4, 2048, 4096], P(None, 'seq', 'mdl'), may hold values from -0.125 to 0.125
- down_weight: bfloat16 [4, 2048, 4096], P(None, 'seq', 'mdl'), may hold values from -0.09375 to 0.09375
Outputs:
- features: bfloat16 [8, 64, 2048], P(('grp', 'mdl'), 'seq'), parts along dimension 0
There are 2 independent parts, one for each index of `grp`. A program takes and returns all parts, laid end to end along the dimension named above; an argument that names none is the same for every part. Nothing has to cross between parts.
Inputs may be any that keep to these rules, and one draw needn't show every extreme that they name: `lengths`: live windows of each recording; one recording is live for all 64, and all recordings together have (320) // 2.
All inputs are finite; a program needn't handle non-finite values.
Results may differ from a plain program's by a relative error of at most 0.014.
Values may be sent and summed in bfloat16 or wider, within the bound.
A program may use at most 128 MiB of HBM per device.

v0:
```python
import math
import jax
import jax.numpy as jnp
from jax import lax
from jax.sharding import PartitionSpec as P

HOP = 128
EPSILON = 1e-06


def shifted(x, axis, by):
    size = lax.axis_size(axis)
    pairs = [(i, i + by) for i in range(size) if 0 <= i + by < size]
    return lax.ppermute(x, axis, pairs)


def spectral_table(half_span):
    full_span = 2 * half_span
    row_index = jnp.arange(full_span, dtype=jnp.int32)
    col_index = jnp.arange(half_span, dtype=jnp.int32)
    phases = row_index[:, None] * col_index[None, :] % full_span
    angles = phases.astype(jnp.float32) * (2.0 * math.pi / full_span)
    window_taper = 0.5 - 0.5 * jnp.cos(row_index.astype(jnp.float32) * (2.0 * math.pi / full_span))
    weighting = window_taper * (1.0 / math.sqrt(full_span))
    joined = jnp.concatenate([jnp.cos(angles), -jnp.sin(angles)], axis=1) * weighting[:, None]
    return jnp.concatenate([joined[:half_span], joined[half_span:]], axis=1)


def log_power(spectrum):
    half_span = spectrum.shape[-1] // 2
    real_part = spectrum[..., :half_span]
    imag_part = spectrum[..., half_span:]
    return jnp.log1p(real_part * real_part + imag_part * imag_part).astype(jnp.bfloat16)


def project_down(hidden, own_down):
    return lax.dot_general(
        hidden, own_down, (((1,), (1,)), ((), ())), preferred_element_type=jnp.float32
    )


def apply_layer(state, up_rows, down_rows, width):
    values = state.astype(jnp.float32)
    squares = lax.psum(jnp.sum(values * values, axis=1, keepdims=True), "seq")
    partial = jnp.dot(state, up_rows, preferred_element_type=jnp.float32).astype(jnp.bfloat16)
    summed = lax.psum_scatter(partial, "seq", scatter_dimension=1, tiled=True)
    scale = lax.rsqrt(squares * (1.0 / width) + EPSILON)
    hidden = jax.nn.gelu(summed.astype(jnp.float32) * scale).astype(jnp.bfloat16)
    hidden = lax.all_gather(hidden, "seq", axis=1, tiled=True)
    added = lax.psum(project_down(hidden, down_rows), "mdl")
    return (values + added).astype(jnp.bfloat16)


def body(signal, lengths, chan_weight, up_weight, down_weight):
    streams, channels, samples = signal.shape
    frames = samples // HOP
    dft_table = spectral_table(HOP)
    boundary = shifted(signal[:, :, :HOP], "seq", -1)
    local_part = jnp.dot(
        signal.reshape(streams, channels, frames, HOP), dft_table, precision=lax.Precision.HIGHEST
    )
    edge_part = jnp.dot(boundary, dft_table[:, 2 * HOP :], precision=lax.Precision.HIGHEST)
    following = jnp.concatenate([local_part[:, :, 1:, 2 * HOP :], edge_part[:, :, None, :]], axis=2)
    spectrum = local_part[..., : 2 * HOP] + following
    logpower = log_power(spectrum)
    embedded = jnp.einsum(
        "scfb,cbe->sfce", logpower, chan_weight, preferred_element_type=jnp.float32
    )
    embedded = embedded.reshape(streams, frames, channels * chan_weight.shape[2])
    frame_index = lax.axis_index("seq") * frames + jnp.arange(frames, dtype=jnp.int32)
    live_mask = frame_index[None, :] < lengths[:, None]
    tokens = jnp.where(live_mask[:, :, None], embedded, 0.0).astype(jnp.bfloat16)
    rows = lax.all_gather(tokens.reshape(streams * frames, -1), "mdl", axis=1, tiled=True)
    state = lax.all_to_all(rows, "seq", split_axis=1, concat_axis=0, tiled=True)
    width = rows.shape[1]
    for layer in range(up_weight.shape[0]):
        state = apply_layer(state, up_weight[layer], down_weight[layer], width)
    rows = lax.all_to_all(state, "seq", split_axis=0, concat_axis=1, tiled=True)
    full_rows = rows.reshape(streams, frames, width)
    half_streams = streams // lax.axis_size("mdl")
    return lax.dynamic_slice_in_dim(
        full_rows, lax.axis_index("mdl") * half_streams, half_streams, 0
    )


def solution(mesh):
    return jax.shard_map(
        body,
        mesh=mesh,
        in_specs=(
            P("grp", "mdl", "seq"),
            P("grp"),
            P("mdl", None, None),
            P(None, "seq", "mdl"),
            P(None, "seq", "mdl"),
        ),
        out_specs=P(("grp", "mdl"), "seq", None),
        check_vma=False,
    )
```

profile of v0, /device:TPU:0, one launch (start us, length us, event | category | flops | bytes accessed | tf_op | source)
XLA Modules:
  0.0 576.4 jit_solution(18243975974515709880)
XLA Ops:
  6.5 1.0 slice.49
  7.5 1.3 collective-permute-start
  8.8 0.5 sine_negate_fusion
  9.5 4.7 convolution_bitcast_fusion
  14.3 1.9 copy-done.1
  16.7 0.4 convolution_bitcast_fusion.2
  17.1 1.9 slice_add_fusion
  19.0 0.4 fusion.4
  19.4 0.4 convolution_bitcast_fusion.1
  19.9 0.2 copy.22
  20.1 0.8 reshape.60
  20.9 2.0 all_gather.15
  22.9 15.4 %all_to_all.35 = bf16[32,8,256]{2,0,1:T(8,128)(2,1)S(1)} all-to-all(bf16[32,8,256]{2,0,1:T(8,128)(2,1)S(1)} %bitcast.87), channel_id=1, replica_groups=mesh['grp'=2,'seq'=8,'mdl'=2] {'seq'}, dimensions={1} | all-to-all | bytes 262144 | tf_op jit(solution)/shard_map/all_to_all | solution.py:74
  38.4 2.7 convolution_convert_fusion.3
  41.3 18.6 %psum.56 = f32[256,1]{0,1:T(1,128)S(1)} all-reduce(f32[256,1]{0,1:T(1,128)S(1)} %broadcast_in_dim.36), channel_id=1, replica_groups=mesh['grp'=2,'seq'=8,'mdl'=2] {'seq'}, use_global_device_ids=true, to_apply=%region_2.3 | all-reduce | flops 256 | bytes 2048 | tf_op jit(solution)/shard_map/psum | solution.py:44
  59.9 43.4 %reduce-scatter.5.cloned.1.call-done = bf16[256,256]{1,0:T(8,128)(2,1)} async-done(((bf16[256,2048]{1,0:T(8,128)(2,1)}), bf16[256,256]{1,0:T(8,128)(2,1)}) %reduce-scatter.5.cloned.1.call-update) | async-done | bytes 131088 | tf_op jit(solution)/shard_map/reduce_scatter | solution.py:46
  103.2 1.7 fusion.39
  105.0 39.1 %all-gather.5.cloned.1.call-done = bf16[256,2048]{1,0:T(8,128)(2,1)} async-done(((bf16[256,256]{1,0:T(8,128)(2,1)}), bf16[256,2048]{1,0:T(8,128)(2,1)}) %all-gather.5.cloned.1.call-update) | async-done | bytes 1048592 | tf_op jit(solution)/shard_map/all_gather | solution.py:49
  144.1 2.7 fusion.14
  146.9 17.3 %all-reduce.5.cloned.1.call-done = f32[256,256]{1,0:T(8,128)} async-done(((f32[256,256]{1,0:T(8,128)}), f32[256,256]{1,0:T(8,128)}) %all-reduce.5.cloned.1.call-update) | async-done | bytes 262160 | tf_op jit(solution)/shard_map/psum | solution.py:50
  164.2 1.1 fusion.26
  165.2 2.7 convolution_convert_fusion.2
  168.0 21.7 %psum.58 = f32[256,1]{0,1:T(1,128)S(1)} all-reduce(f32[256,1]{0,1:T(1,128)S(1)} %bitcast.88), channel_id=1, replica_groups=mesh['grp'=2,'seq'=8,'mdl'=2] {'seq'}, use_global_device_ids=true, to_apply=%region_6.7 | all-reduce | flops 256 | bytes 2048 | tf_op jit(solution)/shard_map/psum | solution.py:44
  189.7 43.6 %reduce-scatter.7.cloned.1.call-done = bf16[256,256]{1,0:T(8,128)(2,1)} async-done(((bf16[256,2048]{1,0:T(8,128)(2,1)}), bf16[256,256]{1,0:T(8,128)(2,1)}) %reduce-scatter.7.cloned.1.call-update) | async-done | bytes 131088 | tf_op jit(solution)/shard_map/reduce_scatter | solution.py:46
  233.3 1.7 fusion.47
  235.1 38.8 %all-gather.7.cloned.1.call-done = bf16[256,2048]{1,0:T(8,128)(2,1)} async-done(((bf16[256,256]{1,0:T(8,128)(2,1)}), bf16[256,2048]{1,0:T(8,128)(2,1)}) %all-gather.7.cloned.1.call-update) | async-done | bytes 1048592 | tf_op jit(solution)/shard_map/all_gather | solution.py:49
  273.9 2.7 fusion.11
  276.7 17.3 %all-reduce.7.cloned.1.call-done = f32[256,256]{1,0:T(8,128)} async-done(((f32[256,256]{1,0:T(8,128)}), f32[256,256]{1,0:T(8,128)}) %all-reduce.7.cloned.1.call-update) | async-done | bytes 262160 | tf_op jit(solution)/shard_map/psum | solution.py:50
  294.0 1.1 fusion.28
  295.0 2.7 convolution_convert_fusion.1
  297.8 21.7 %psum.60 = f32[256,1]{0,1:T(1,128)S(1)} all-reduce(f32[256,1]{0,1:T(1,128)S(1)} %bitcast.89), channel_id=1, replica_groups=mesh['grp'=2,'seq'=8,'mdl'=2] {'seq'}, use_global_device_ids=true, to_apply=%region_10.11 | all-reduce | flops 256 | bytes 2048 | tf_op jit(solution)/shard_map/psum | solution.py:44
  319.5 43.6 %reduce-scatter.9.cloned.1.call-done = bf16[256,256]{1,0:T(8,128)(2,1)} async-done(((bf16[256,2048]{1,0:T(8,128)(2,1)}), bf16[256,256]{1,0:T(8,128)(2,1)}) %reduce-scatter.9.cloned.1.call-update) | async-done | bytes 131088 | tf_op jit(solution)/shard_map/reduce_scatter | solution.py:46
  363.1 1.7 fusion.55
  364.9 39.0 %all-gather.9.cloned.1.call-done = bf16[256,2048]{1,0:T(8,128)(2,1)} async-done(((bf16[256,256]{1,0:T(8,128)(2,1)}), bf16[256,2048]{1,0:T(8,128)(2,1)}) %all-gather.9.cloned.1.call-update) | async-done | bytes 1048592 | tf_op jit(solution)/shard_map/all_gather | solution.py:49
  403.9 2.7 fusion.8
  406.7 17.3 %all-reduce.9.cloned.1.call-done = f32[256,256]{1,0:T(8,128)} async-done(((f32[256,256]{1,0:T(8,128)}), f32[256,256]{1,0:T(8,128)}) %all-reduce.9.cloned.1.call-update) | async-done | bytes 262160 | tf_op jit(solution)/shard_map/psum | solution.py:50
  423.9 1.1 fusion.30
  425.0 2.7 convolution_convert_fusion
  427.7 21.7 %psum.62 = f32[256,1]{0,1:T(1,128)S(1)} all-reduce(f32[256,1]{0,1:T(1,128)S(1)} %bitcast.90), channel_id=1, replica_groups=mesh['grp'=2,'seq'=8,'mdl'=2] {'seq'}, use_global_device_ids=true, to_apply=%region_14.15 | all-reduce | flops 256 | bytes 2048 | tf_op jit(solution)/shard_map/psum | solution.py:44
  449.4 43.6 %reduce-scatter.11.cloned.1.call-done = bf16[256,256]{1,0:T(8,128)(2,1)} async-done(((bf16[256,2048]{1,0:T(8,128)(2,1)}), bf16[256,256]{1,0:T(8,128)(2,1)}) %reduce-scatter.11.cloned.1.call-update) | async-done | bytes 131088 | tf_op jit(solution)/shard_map/reduce_scatter | solution.py:46
  493.0 1.7 fusion.63
  494.8 39.0 %all-gather.11.cloned.1.call-done = bf16[256,2048]{1,0:T(8,128)(2,1)} async-done(((bf16[256,256]{1,0:T(8,128)(2,1)}), bf16[256,2048]{1,0:T(8,128)(2,1)}) %all-gather.11.cloned.1.call-update) | async-done | bytes 1048592 | tf_op jit(solution)/shard_map/all_gather | solution.py:49
  533.8 2.7 fusion.5
  536.6 17.3 %all-reduce.11.cloned.1.call-done = f32[256,256]{1,0:T(8,128)} async-done(((f32[256,256]{1,0:T(8,128)}), f32[256,256]{1,0:T(8,128)}) %all-reduce.11.cloned.1.call-update) | async-done | bytes 262160 | tf_op jit(solution)/shard_map/psum | solution.py:50
  553.9 1.6 fusion.31
  555.5 5.8 %all-to-all-start.1 = ((bf16[8,32,256]{2,1,0:T(8,128)(2,1)}), bf16[8,32,256]{2,1,0:T(8,128)(2,1)S(1)}, u32[]{:S(2)}, u32[]{:S(2)}) async-start(bf16[8,32,256]{2,1,0:T(8,128)(2,1)} %bitcast.27), calls=%async_computation.5 | async-start | bytes 262144 | tf_op jit(solution)/shard_map/all_to_all | solution.py:78
  561.3 7.4 %all-to-all-done.1 = bf16[8,32,256]{2,1,0:T(8,128)(2,1)S(1)} async-done(((bf16[8,32,256]{2,1,0:T(8,128)(2,1)}), bf16[8,32,256]{2,1,0:T(8,128)(2,1)S(1)}, u32[]{:S(2)}, u32[]{:S(2)}) %all-to-all-start.1) | async-done | bytes 131104 | tf_op jit(solution)/shard_map/all_to_all | solution.py:78
  568.9 0.6 constant_dynamic-slice_fusion
  (50 shorter events, 1.8 us)
Async XLA Ops:
  6.5 12.9 %copy-start = (bf16[64,128,16]{1,2,0:T(8,128)(2,1)S(1)}, bf16[64,128,16]{1,2,0:T(8,128)(2,1)}, u32[]{:S(2)}) copy-start(bf16[64,128,16]{1,2,0:T(8,128)(2,1)} %param.7) | copy-start | bytes 786436
  6.5 96.7 %reduce-scatter.5.cloned.1.call-start = ((), (), s32[]{:S(2)}) async-start(), calls=%async_computation.6 | async-start | bytes 1179648 | tf_op jit(solution)/shard_map/reduce_scatter | solution.py:46
  7.5 9.2 %collective-permute-start = (f32[4,64,128]{2,1,0:T(8,128)S(1)}, f32[4,64,128]{2,1,0:T(8,128)S(1)}, u32[]{:S(2)}, u32[]{:S(2)}) collective-permute-start(f32[4,64,128]{2,1,0:T(8,128)S(1)} %slice.49), channel_id=1, source_target_pairs={{2,0},{4,2},{6,4},{8,6},{10,8},{12,10},{14,12},{3,1},{5,3},{7,5},{... | collective-permute-start | bytes 393224 | tf_op jit(solution)/shard_map/ppermute | solution.py:14
  9.5 7.0 %copy-start.2 = (s32[4]{0:T(128)S(1)}, s32[4]{0:T(128)}, u32[]{:S(2)}) copy-start(s32[4]{0:T(128)} %param.6) | copy-start | bytes 52
  14.3 1.9 copy-start.1
  41.0 103.1 %all-gather.5.cloned.1.call-start = ((), (), s32[]{:S(2)}) async-start(), calls=%async_computation.7 | async-start | bytes 1179648 | tf_op jit(solution)/shard_map/all_gather | solution.py:49
  105.0 59.2 %all-reduce.5.cloned.1.call-start = ((), (), s32[]{:S(2)}) async-start(), calls=%async_computation.8 | async-start | bytes 524288 | tf_op jit(solution)/shard_map/psum | solution.py:50
  146.9 86.4 %reduce-scatter.7.cloned.1.call-start = ((), (), s32[]{:S(2)}) async-start(), calls=%async_computation.9 | async-start | bytes 1179648 | tf_op jit(solution)/shard_map/reduce_scatter | solution.py:46
  167.9 106.0 %all-gather.7.cloned.1.call-start = ((), (), s32[]{:S(2)}) async-start(), calls=%async_computation.10 | async-start | bytes 1179648 | tf_op jit(solution)/shard_map/all_gather | solution.py:49
  235.0 59.0 %all-reduce.7.cloned.1.call-start = ((), (), s32[]{:S(2)}) async-start(), calls=%async_computation.11 | async-start | bytes 524288 | tf_op jit(solution)/shard_map/psum | solution.py:50
  276.7 86.4 %reduce-scatter.9.cloned.1.call-start = ((), (), s32[]{:S(2)}) async-start(), calls=%async_computation.12 | async-start | bytes 1179648 | tf_op jit(solution)/shard_map/reduce_scatter | solution.py:46
  297.7 106.1 %all-gather.9.cloned.1.call-start = ((), (), s32[]{:S(2)}) async-start(), calls=%async_computation.13 | async-start | bytes 1179648 | tf_op jit(solution)/shard_map/all_gather | solution.py:49
  364.8 59.1 %all-reduce.9.cloned.1.call-start = ((), (), s32[]{:S(2)}) async-start(), calls=%async_computation.14 | async-start | bytes 524288 | tf_op jit(solution)/shard_map/psum | solution.py:50
  406.6 86.4 %reduce-scatter.11.cloned.1.call-start = ((), (), s32[]{:S(2)}) async-start(), calls=%async_computation.15 | async-start | bytes 1179648 | tf_op jit(solution)/shard_map/reduce_scatter | solution.py:46
  427.7 106.2 %all-gather.11.cloned.1.call-start = ((), (), s32[]{:S(2)}) async-start(), calls=%async_computation.16 | async-start | bytes 1179648 | tf_op jit(solution)/shard_map/all_gather | solution.py:49
  494.8 59.1 %all-reduce.11.cloned.1.call-start = ((), (), s32[]{:S(2)}) async-start(), calls=%async_computation.17 | async-start | bytes 524288 | tf_op jit(solution)/shard_map/psum | solution.py:50
  555.5 13.2 %all-to-all-start.1 = ((bf16[8,32,256]{2,1,0:T(8,128)(2,1)}), bf16[8,32,256]{2,1,0:T(8,128)(2,1)S(1)}, u32[]{:S(2)}, u32[]{:S(2)}) async-start(bf16[8,32,256]{2,1,0:T(8,128)(2,1)} %bitcast.27), calls=%async_computation.5 | async-start | bytes 262144 | tf_op jit(solution)/shard_map/all_to_all | solution.py:78
Sparse Core Ops, SparseCore 0:
  41.2 62.0 reduce-scatter.4
  105.5 38.5 all-gather.4
  147.0 17.1 all-reduce.4
  168.0 65.1 reduce-scatter.6
  235.3 38.5 all-gather.6
  276.8 17.1 all-reduce.6
  297.8 65.1 reduce-scatter.8
  365.3 38.5 all-gather.8
  406.7 17.1 all-reduce.8
  427.8 65.1 reduce-scatter.10
  495.3 38.5 all-gather.10
  536.7 17.1 all-reduce.10
where the time goes:
time: 577 us; the launch traced here: 576 us
  waiting for transfers between devices  407 us (71%)
  blocking collectives  101 us (18%)
  matrix products  27.1 us (5%)
  other arithmetic  15 us (3%)
  between operations  13.7 us (2%)
  starting transfers between devices  7.53 us (1%)
    reduce_scatter x4, waiting for transfers between devices, apply_layer(): summed = lax.psum_scatter(partial, 'seq', scatter_dimension=1, tiled=True)  174 us
    all_gather x4, waiting for transfers between devices, apply_layer(): hidden = lax.all_gather(hidden, 'seq', axis=1, tiled=True)  156 us
    psum x4, blocking collectives, apply_layer(): squares = lax.psum(jnp.sum(values * values, axis=1, keepdims=True), 'seq')  83.7 us
    psum x4, waiting for transfers between devices, apply_layer(): added = lax.psum(project_down(hidden, down_rows), 'mdl')  69.1 us
    all_to_all x1, blocking collectives, body(): state = lax.all_to_all(rows, 'seq', split_axis=1, concat_axis=0, tiled=True)  15.4 us
  transfers between devices with their start and end apart: 14, of which 13 were waited for; matrix products, arithmetic and copies ran while one was open for 1% of the time, Pallas kernels for 0%

commit v1 on v0

--- a/solution.py
+++ b/solution.py
@@ -46,7 +46,12 @@
     summed = lax.psum_scatter(partial, "seq", scatter_dimension=1, tiled=True)
     scale = lax.rsqrt(squares * (1.0 / width) + EPSILON)
     hidden = jax.nn.gelu(summed.astype(jnp.float32) * scale).astype(jnp.bfloat16)
-    hidden = lax.all_gather(hidden, "seq", axis=1, tiled=True)
+    ring = [hidden]
+    for hop in range(7):
+        ring.append(lax.ppermute(ring[-1], "seq", [(dev, (dev + 1) % 8) for dev in range(8)]))
+    hidden = jnp.roll(
+        jnp.concatenate(ring[::-1], axis=1), (lax.axis_index("seq") + 1) * ring[0].shape[1], axis=1
+    )
     added = lax.psum(project_down(hidden, down_rows), "mdl")
     return (values + added).astype(jnp.bfloat16)
 

time: 577 us -> 633 us (1.097)
  waiting for transfers between devices: 407 us -> 461 us
    ppermute x0 -> x28, waiting for transfers between devices: none -> 216 us  [apply_layer(): lax.ppermute(ring[-1], 'seq', [(dev, (dev + 1) % 8) for dev in range(8)])]
    all_gather x4 -> x0, waiting for transfers between devices: 156 us -> none  [apply_layer(): hidden = lax.all_gather(hidden, 'seq', axis=1, tiled=True)]
    psum x4, waiting for transfers between devices: 69.1 us -> 62.5 us  [apply_layer(): added = lax.psum(project_down(hidden, down_rows), 'mdl')]
  transfers between devices with their start and end apart: 14 -> 38, of which waited for: 13 -> 38; matrix products, arithmetic and copies ran while one was open for 1% -> 1% of each run, Pallas kernels for 0% -> 0%
where the time goes in v1:
time: 633 us; the launch traced here: 632 us
  waiting for transfers between devices  461 us (73%)
  blocking collectives  101 us (16%)
  matrix products  25.6 us (4%)
  between operations  14 us (2%)
  other arithmetic  13.3 us (2%)
  starting transfers between devices  12.5 us (2%)
    ppermute x28, waiting for transfers between devices, apply_layer(): lax.ppermute(ring[-1], 'seq', [(dev, (dev + 1) % 8) for dev in range(8)])  216 us
    reduce_scatter x4, waiting for transfers between devices, apply_layer(): summed = lax.psum_scatter(partial, 'seq', scatter_dimension=1, tiled=True)  174 us
    psum x4, blocking collectives, apply_layer(): squares = lax.psum(jnp.sum(values * values, axis=1, keepdims=True), 'seq')  83.7 us
    psum x4, waiting for transfers between devices, apply_layer(): added = lax.psum(project_down(hidden, down_rows), 'mdl')  62.5 us
    all_to_all x1, blocking collectives, body(): state = lax.all_to_all(rows, 'seq', split_axis=1, concat_axis=0, tiled=True)  15.2 us
  transfers between devices with their start and end apart: 38, of which 38 were waited for; matrix products, arithmetic and copies ran while one was open for 1% of the time, Pallas kernels for 0%

profile of v1, /device:TPU:0, one launch (start us, length us, event | category | flops | bytes accessed | tf_op | source)
XLA Modules:
  0.0 632.4 jit_solution(7901543129248118074)
XLA Ops:
  9.6 3.5 convolution_bitcast_fusion
  22.1 15.2 %all_to_all.35 = bf16[32,8,256]{2,0,1:T(8,128)(2,1)S(1)} all-to-all(bf16[32,8,256]{2,0,1:T(8,128)(2,1)S(1)} %bitcast.83), channel_id=1, replica_groups=mesh['grp'=2,'seq'=8,'mdl'=2] {'seq'}, dimensions={1} | all-to-all | bytes 262144 | tf_op jit(solution)/shard_map/all_to_all | solution.py:79
  37.3 2.7 convolution_convert_fusion.3
  40.2 18.6 %psum.56 = f32[256,1]{0,1:T(1,128)S(1)} all-reduce(f32[256,1]{0,1:T(1,128)S(1)} %broadcast_in_dim.36), channel_id=1, replica_groups=mesh['grp'=2,'seq'=8,'mdl'=2] {'seq'}, use_global_device_ids=true, to_apply=%region_2.3 | all-reduce | flops 256 | bytes 2048 | tf_op jit(solution)/shard_map/psum | solution.py:44
  58.8 43.2 %reduce-scatter.5.cloned.1.call-done = bf16[256,256]{1,0:T(8,128)(2,1)} async-done(((bf16[256,2048]{1,0:T(8,128)(2,1)}), bf16[256,256]{1,0:T(8,128)(2,1)}) %reduce-scatter.5.cloned.1.call-update) | async-done | bytes 131088 | tf_op jit(solution)/shard_map/reduce_scatter | solution.py:46
  104.5 6.3 %collective-permute-done.1 = bf16[256,256]{1,0:T(8,128)(2,1)S(1)} collective-permute-done((bf16[256,256]{1,0:T(8,128)(2,1)S(1)}, bf16[256,256]{1,0:T(8,128)(2,1)S(1)}, u32[]{:S(2)}, u32[]{:S(2)}) %collective-permute-start.1) | collective-permute-done | bytes 131104 | tf_op jit(solution)/shard_map/ppermute | solution.py:51
  110.9 7.7 %collective-permute-done.2 = bf16[256,256]{1,0:T(8,128)(2,1)S(1)} collective-permute-done((bf16[256,256]{1,0:T(8,128)(2,1)S(1)}, bf16[256,256]{1,0:T(8,128)(2,1)S(1)}, u32[]{:S(2)}, u32[]{:S(2)}) %collective-permute-start.2) | collective-permute-done | bytes 131104 | tf_op jit(solution)/shard_map/ppermute | solution.py:51
  118.6 7.7 %collective-permute-done.3 = bf16[256,256]{1,0:T(8,128)(2,1)S(1)} collective-permute-done((bf16[256,256]{1,0:T(8,128)(2,1)S(1)}, bf16[256,256]{1,0:T(8,128)(2,1)S(1)}, u32[]{:S(2)}, u32[]{:S(2)}) %collective-permute-start.3) | collective-permute-done | bytes 131104 | tf_op jit(solution)/shard_map/ppermute | solution.py:51
  126.2 8.7 %collective-permute-done.4 = bf16[256,256]{1,0:T(8,128)(2,1)S(1)} collective-permute-done((bf16[256,256]{1,0:T(8,128)(2,1)S(1)}, bf16[256,256]{1,0:T(8,128)(2,1)S(1)}, u32[]{:S(2)}, u32[]{:S(2)}) %collective-permute-start.4) | collective-permute-done | bytes 131104 | tf_op jit(solution)/shard_map/ppermute | solution.py:51
  135.0 8.3 %collective-permute-done.5 = bf16[256,256]{1,0:T(8,128)(2,1)S(1)} collective-permute-done((bf16[256,256]{1,0:T(8,128)(2,1)S(1)}, bf16[256,256]{1,0:T(8,128)(2,1)S(1)}, u32[]{:S(2)}, u32[]{:S(2)}) %collective-permute-start.5) | collective-permute-done | bytes 131104 | tf_op jit(solution)/shard_map/ppermute | solution.py:51
  143.2 7.7 %collective-permute-done.6 = bf16[256,256]{1,0:T(8,128)(2,1)S(1)} collective-permute-done((bf16[256,256]{1,0:T(8,128)(2,1)S(1)}, bf16[256,256]{1,0:T(8,128)(2,1)S(1)}, u32[]{:S(2)}, u32[]{:S(2)}) %collective-permute-start.6) | collective-permute-done | bytes 131104 | tf_op jit(solution)/shard_map/ppermute | solution.py:51
  150.9 7.7 %collective-permute-done.7 = bf16[256,256]{1,0:T(8,128)(2,1)S(1)} collective-permute-done((bf16[256,256]{1,0:T(8,128)(2,1)S(1)}, bf16[256,256]{1,0:T(8,128)(2,1)S(1)}, u32[]{:S(2)}, u32[]{:S(2)}) %collective-permute-start.7) | collective-permute-done | bytes 131104 | tf_op jit(solution)/shard_map/ppermute | solution.py:51
  161.6 15.6 %all-reduce.5.cloned.1.call-done = f32[256,256]{1,0:T(8,128)} async-done(((f32[256,256]{1,0:T(8,128)}), f32[256,256]{1,0:T(8,128)}) %all-reduce.5.cloned.1.call-update) | async-done | bytes 262160 | tf_op jit(solution)/shard_map/psum | solution.py:55
  178.3 2.7 convolution_convert_fusion.2
  181.0 21.7 %psum.58 = f32[256,1]{0,1:T(1,128)S(1)} all-reduce(f32[256,1]{0,1:T(1,128)S(1)} %bitcast.92), channel_id=1, replica_groups=mesh['grp'=2,'seq'=8,'mdl'=2] {'seq'}, use_global_device_ids=true, to_apply=%region_6.8 | all-reduce | flops 256 | bytes 2048 | tf_op jit(solution)/shard_map/psum | solution.py:44
  202.7 43.6 %reduce-scatter.7.cloned.1.call-done = bf16[256,256]{1,0:T(8,128)(2,1)} async-done(((bf16[256,2048]{1,0:T(8,128)(2,1)}), bf16[256,256]{1,0:T(8,128)(2,1)}) %reduce-scatter.7.cloned.1.call-update) | async-done | bytes 131088 | tf_op jit(solution)/shard_map/reduce_scatter | solution.py:46
  248.7 6.5 %collective-permute-done.8 = bf16[256,256]{1,0:T(8,128)(2,1)S(1)} collective-permute-done((bf16[256,256]{1,0:T(8,128)(2,1)S(1)}, bf16[256,256]{1,0:T(8,128)(2,1)S(1)}, u32[]{:S(2)}, u32[]{:S(2)}) %collective-permute-start.8) | collective-permute-done | bytes 131104 | tf_op jit(solution)/shard_map/ppermute | solution.py:51
  255.2 7.7 %collective-permute-done.9 = bf16[256,256]{1,0:T(8,128)(2,1)S(1)} collective-permute-done((bf16[256,256]{1,0:T(8,128)(2,1)S(1)}, bf16[256,256]{1,0:T(8,128)(2,1)S(1)}, u32[]{:S(2)}, u32[]{:S(2)}) %collective-permute-start.9) | collective-permute-done | bytes 131104 | tf_op jit(solution)/shard_map/ppermute | solution.py:51
  262.8 7.7 %collective-permute-done.10 = bf16[256,256]{1,0:T(8,128)(2,1)S(1)} collective-permute-done((bf16[256,256]{1,0:T(8,128)(2,1)S(1)}, bf16[256,256]{1,0:T(8,128)(2,1)S(1)}, u32[]{:S(2)}, u32[]{:S(2)}) %collective-permute-start.10) | collective-permute-done | bytes 131104 | tf_op jit(solution)/shard_map/ppermute | solution.py:51
  270.5 8.8 %collective-permute-done.11 = bf16[256,256]{1,0:T(8,128)(2,1)S(1)} collective-permute-done((bf16[256,256]{1,0:T(8,128)(2,1)S(1)}, bf16[256,256]{1,0:T(8,128)(2,1)S(1)}, u32[]{:S(2)}, u32[]{:S(2)}) %collective-permute-start.11) | collective-permute-done | bytes 131104 | tf_op jit(solution)/shard_map/ppermute | solution.py:51
  279.3 8.2 %collective-permute-done.12 = bf16[256,256]{1,0:T(8,128)(2,1)S(1)} collective-permute-done((bf16[256,256]{1,0:T(8,128)(2,1)S(1)}, bf16[256,256]{1,0:T(8,128)(2,1)S(1)}, u32[]{:S(2)}, u32[]{:S(2)}) %collective-permute-start.12) | collective-permute-done | bytes 131104 | tf_op jit(solution)/shard_map/ppermute | solution.py:51
  287.5 7.7 %collective-permute-done.13 = bf16[256,256]{1,0:T(8,128)(2,1)S(1)} collective-permute-done((bf16[256,256]{1,0:T(8,128)(2,1)S(1)}, bf16[256,256]{1,0:T(8,128)(2,1)S(1)}, u32[]{:S(2)}, u32[]{:S(2)}) %collective-permute-start.13) | collective-permute-done | bytes 131104 | tf_op jit(solution)/shard_map/ppermute | solution.py:51
  295.2 7.7 %collective-permute-done.14 = bf16[256,256]{1,0:T(8,128)(2,1)S(1)} collective-permute-done((bf16[256,256]{1,0:T(8,128)(2,1)S(1)}, bf16[256,256]{1,0:T(8,128)(2,1)S(1)}, u32[]{:S(2)}, u32[]{:S(2)}) %collective-permute-start.14) | collective-permute-done | bytes 131104 | tf_op jit(solution)/shard_map/ppermute | solution.py:51
  305.9 15.6 %all-reduce.7.cloned.1.call-done = f32[256,256]{1,0:T(8,128)} async-done(((f32[256,256]{1,0:T(8,128)}), f32[256,256]{1,0:T(8,128)}) %all-reduce.7.cloned.1.call-update) | async-done | bytes 262160 | tf_op jit(solution)/shard_map/psum | solution.py:55
  322.5 2.7 convolution_convert_fusion.1
  325.3 21.7 %psum.60 = f32[256,1]{0,1:T(1,128)S(1)} all-reduce(f32[256,1]{0,1:T(1,128)S(1)} %bitcast.93), channel_id=1, replica_groups=mesh['grp'=2,'seq'=8,'mdl'=2] {'seq'}, use_global_device_ids=true, to_apply=%region_10.12 | all-reduce | flops 256 | bytes 2048 | tf_op jit(solution)/shard_map/psum | solution.py:44
  347.0 43.5 %reduce-scatter.9.cloned.1.call-done = bf16[256,256]{1,0:T(8,128)(2,1)} async-done(((bf16[256,2048]{1,0:T(8,128)(2,1)}), bf16[256,256]{1,0:T(8,128)(2,1)}) %reduce-scatter.9.cloned.1.call-update) | async-done | bytes 131088 | tf_op jit(solution)/shard_map/reduce_scatter | solution.py:46
  392.8 6.5 %collective-permute-done.15 = bf16[256,256]{1,0:T(8,128)(2,1)S(1)} collective-permute-done((bf16[256,256]{1,0:T(8,128)(2,1)S(1)}, bf16[256,256]{1,0:T(8,128)(2,1)S(1)}, u32[]{:S(2)}, u32[]{:S(2)}) %collective-permute-start.15) | collective-permute-done | bytes 131104 | tf_op jit(solution)/shard_map/ppermute | solution.py:51
  399.3 7.7 %collective-permute-done.16 = bf16[256,256]{1,0:T(8,128)(2,1)S(1)} collective-permute-done((bf16[256,256]{1,0:T(8,128)(2,1)S(1)}, bf16[256,256]{1,0:T(8,128)(2,1)S(1)}, u32[]{:S(2)}, u32[]{:S(2)}) %collective-permute-start.16) | collective-permute-done | bytes 131104 | tf_op jit(solution)/shard_map/ppermute | solution.py:51
  407.0 7.7 %collective-permute-done.17 = bf16[256,256]{1,0:T(8,128)(2,1)S(1)} collective-permute-done((bf16[256,256]{1,0:T(8,128)(2,1)S(1)}, bf16[256,256]{1,0:T(8,128)(2,1)S(1)}, u32[]{:S(2)}, u32[]{:S(2)}) %collective-permute-start.17) | collective-permute-done | bytes 131104 | tf_op jit(solution)/shard_map/ppermute | solution.py:51
  414.7 8.8 %collective-permute-done.18 = bf16[256,256]{1,0:T(8,128)(2,1)S(1)} collective-permute-done((bf16[256,256]{1,0:T(8,128)(2,1)S(1)}, bf16[256,256]{1,0:T(8,128)(2,1)S(1)}, u32[]{:S(2)}, u32[]{:S(2)}) %collective-permute-start.18) | collective-permute-done | bytes 131104 | tf_op jit(solution)/shard_map/ppermute | solution.py:51
  423.4 8.2 %collective-permute-done.19 = bf16[256,256]{1,0:T(8,128)(2,1)S(1)} collective-permute-done((bf16[256,256]{1,0:T(8,128)(2,1)S(1)}, bf16[256,256]{1,0:T(8,128)(2,1)S(1)}, u32[]{:S(2)}, u32[]{:S(2)}) %collective-permute-start.19) | collective-permute-done | bytes 131104 | tf_op jit(solution)/shard_map/ppermute | solution.py:51
  431.7 7.7 %collective-permute-done.20 = bf16[256,256]{1,0:T(8,128)(2,1)S(1)} collective-permute-done((bf16[256,256]{1,0:T(8,128)(2,1)S(1)}, bf16[256,256]{1,0:T(8,128)(2,1)S(1)}, u32[]{:S(2)}, u32[]{:S(2)}) %collective-permute-start.20) | collective-permute-done | bytes 131104 | tf_op jit(solution)/shard_map/ppermute | solution.py:51
  439.3 7.7 %collective-permute-done.21 = bf16[256,256]{1,0:T(8,128)(2,1)S(1)} collective-permute-done((bf16[256,256]{1,0:T(8,128)(2,1)S(1)}, bf16[256,256]{1,0:T(8,128)(2,1)S(1)}, u32[]{:S(2)}, u32[]{:S(2)}) %collective-permute-start.21) | collective-permute-done | bytes 131104 | tf_op jit(solution)/shard_map/ppermute | solution.py:51
  450.0 15.6 %all-reduce.9.cloned.1.call-done = f32[256,256]{1,0:T(8,128)} async-done(((f32[256,256]{1,0:T(8,128)}), f32[256,256]{1,0:T(8,128)}) %all-reduce.9.cloned.1.call-update) | async-done | bytes 262160 | tf_op jit(solution)/shard_map/psum | solution.py:55
  466.7 2.7 convolution_convert_fusion
  469.4 21.7 %psum.62 = f32[256,1]{0,1:T(1,128)S(1)} all-reduce(f32[256,1]{0,1:T(1,128)S(1)} %bitcast.94), channel_id=1, replica_groups=mesh['grp'=2,'seq'=8,'mdl'=2] {'seq'}, use_global_device_ids=true, to_apply=%region_14.16 | all-reduce | flops 256 | bytes 2048 | tf_op jit(solution)/shard_map/psum | solution.py:44
  491.1 43.6 %reduce-scatter.11.cloned.1.call-done = bf16[256,256]{1,0:T(8,128)(2,1)} async-done(((bf16[256,2048]{1,0:T(8,128)(2,1)}), bf16[256,256]{1,0:T(8,128)(2,1)}) %reduce-scatter.11.cloned.1.call-update) | async-done | bytes 131088 | tf_op jit(solution)/shard_map/reduce_scatter | solution.py:46
  537.1 6.5 %collective-permute-done.22 = bf16[256,256]{1,0:T(8,128)(2,1)S(1)} collective-permute-done((bf16[256,256]{1,0:T(8,128)(2,1)S(1)}, bf16[256,256]{1,0:T(8,128)(2,1)S(1)}, u32[]{:S(2)}, u32[]{:S(2)}) %collective-permute-start.22) | collective-permute-done | bytes 131104 | tf_op jit(solution)/shard_map/ppermute | solution.py:51
  543.6 7.7 %collective-permute-done.23 = bf16[256,256]{1,0:T(8,128)(2,1)S(1)} collective-permute-done((bf16[256,256]{1,0:T(8,128)(2,1)S(1)}, bf16[256,256]{1,0:T(8,128)(2,1)S(1)}, u32[]{:S(2)}, u32[]{:S(2)}) %collective-permute-start.23) | collective-permute-done | bytes 131104 | tf_op jit(solution)/shard_map/ppermute | solution.py:51
  551.2 7.7 %collective-permute-done.24 = bf16[256,256]{1,0:T(8,128)(2,1)S(1)} collective-permute-done((bf16[256,256]{1,0:T(8,128)(2,1)S(1)}, bf16[256,256]{1,0:T(8,128)(2,1)S(1)}, u32[]{:S(2)}, u32[]{:S(2)}) %collective-permute-start.24) | collective-permute-done | bytes 131104 | tf_op jit(solution)/shard_map/ppermute | solution.py:51
  558.9 8.8 %collective-permute-done.25 = bf16[256,256]{1,0:T(8,128)(2,1)S(1)} collective-permute-done((bf16[256,256]{1,0:T(8,128)(2,1)S(1)}, bf16[256,256]{1,0:T(8,128)(2,1)S(1)}, u32[]{:S(2)}, u32[]{:S(2)}) %collective-permute-start.25) | collective-permute-done | bytes 131104 | tf_op jit(solution)/shard_map/ppermute | solution.py:51
  567.7 8.2 %collective-permute-done.26 = bf16[256,256]{1,0:T(8,128)(2,1)S(1)} collective-permute-done((bf16[256,256]{1,0:T(8,128)(2,1)S(1)}, bf16[256,256]{1,0:T(8,128)(2,1)S(1)}, u32[]{:S(2)}, u32[]{:S(2)}) %collective-permute-start.26) | collective-permute-done | bytes 131104 | tf_op jit(solution)/shard_map/ppermute | solution.py:51
  575.9 7.7 %collective-permute-done.27 = bf16[256,256]{1,0:T(8,128)(2,1)S(1)} collective-permute-done((bf16[256,256]{1,0:T(8,128)(2,1)S(1)}, bf16[256,256]{1,0:T(8,128)(2,1)S(1)}, u32[]{:S(2)}, u32[]{:S(2)}) %collective-permute-start.27) | collective-permute-done | bytes 131104 | tf_op jit(solution)/shard_map/ppermute | solution.py:51
  583.6 7.7 %collective-permute-done.28 = bf16[256,256]{1,0:T(8,128)(2,1)S(1)} collective-permute-done((bf16[256,256]{1,0:T(8,128)(2,1)S(1)}, bf16[256,256]{1,0:T(8,128)(2,1)S(1)}, u32[]{:S(2)}, u32[]{:S(2)}) %collective-permute-start.28) | collective-permute-done | bytes 131104 | tf_op jit(solution)/shard_map/ppermute | solution.py:51
  594.2 15.7 %all-reduce.11.cloned.1.call-done = f32[256,256]{1,0:T(8,128)} async-done(((f32[256,256]{1,0:T(8,128)}), f32[256,256]{1,0:T(8,128)}) %all-reduce.11.cloned.1.call-update) | async-done | bytes 262160 | tf_op jit(solution)/shard_map/psum | solution.py:55
  611.5 5.8 all-to-all-start.1
  617.3 7.4 %all-to-all-done.1 = bf16[8,32,256]{2,1,0:T(8,128)(2,1)S(1)} async-done(((bf16[8,32,256]{2,1,0:T(8,128)(2,1)}), bf16[8,32,256]{2,1,0:T(8,128)(2,1)S(1)}, u32[]{:S(2)}, u32[]{:S(2)}) %all-to-all-start.1) | async-done | bytes 131104 | tf_op jit(solution)/shard_map/all_to_all | solution.py:83
  (136 shorter events, 39.4 us)
Async XLA Ops:
  6.5 12.1 %copy-start = (bf16[64,128,16]{1,2,0:T(8,128)(2,1)S(1)}, bf16[64,128,16]{1,2,0:T(8,128)(2,1)}, u32[]{:S(2)}) copy-start(bf16[64,128,16]{1,2,0:T(8,128)(2,1)} %param.9) | copy-start | bytes 786436
  6.5 3.0 copy-start.2
  6.5 95.5 %reduce-scatter.5.cloned.1.call-start = ((), (), s32[]{:S(2)}) async-start(), calls=%async_computation.6 | async-start | bytes 1179648 | tf_op jit(solution)/shard_map/reduce_scatter | solution.py:46
  7.6 8.4 %collective-permute-start = (f32[4,64,128]{2,1,0:T(8,128)S(1)}, f32[4,64,128]{2,1,0:T(8,128)S(1)}, u32[]{:S(2)}, u32[]{:S(2)}) collective-permute-start(f32[4,64,128]{2,1,0:T(8,128)S(1)} %slice.49), channel_id=1, source_target_pairs={{2,0},{4,2},{6,4},{8,6},{10,8},{12,10},{14,12},{3,1},{5,3},{7,5},{... | collective-permute-start | bytes 393224 | tf_op jit(solution)/shard_map/ppermute | solution.py:14
  13.1 1.9 copy-start.1
  13.2 2.3 copy-start.7
  40.0 137.2 %all-reduce.5.cloned.1.call-start = ((), (), s32[]{:S(2)}) async-start(), calls=%async_computation.7 | async-start | bytes 524288 | tf_op jit(solution)/shard_map/psum | solution.py:55
  102.0 56.6 %copy-start.3 = (bf16[256,256]{1,0:T(8,128)(2,1)S(1)}, bf16[256,256]{1,0:T(8,128)(2,1)}, u32[]{:S(2)}) copy-start(bf16[256,256]{1,0:T(8,128)(2,1)} %reduce-scatter.5.cloned.1.call-done) | copy-start | bytes 393220
  103.2 7.7 %collective-permute-start.1 = (bf16[256,256]{1,0:T(8,128)(2,1)S(1)}, bf16[256,256]{1,0:T(8,128)(2,1)S(1)}, u32[]{:S(2)}, u32[]{:S(2)}) collective-permute-start(bf16[256,256]{1,0:T(8,128)(2,1)S(1)} %fusion.47), channel_id=1, source_target_pairs={{0,2},{2,4},{4,6},{6,8},{8,10},{10,12},{12,14},{14,0},{1,3},{3,5},... | collective-permute-start | bytes 393224 | tf_op jit(solution)/shard_map/ppermute | solution.py:51
  110.9 7.7 %collective-permute-start.2 = (bf16[256,256]{1,0:T(8,128)(2,1)S(1)}, bf16[256,256]{1,0:T(8,128)(2,1)S(1)}, u32[]{:S(2)}, u32[]{:S(2)}) collective-permute-start(bf16[256,256]{1,0:T(8,128)(2,1)S(1)} %collective-permute-done.1), channel_id=1, source_target_pairs={{0,2},{2,4},{4,6},{6,8},{8,10},{10,12},{12,14},{14,0},{1,3},{3,5},... | collective-permute-start | bytes 393224 | tf_op jit(solution)/shard_map/ppermute | solution.py:51
  118.6 7.7 %collective-permute-start.3 = (bf16[256,256]{1,0:T(8,128)(2,1)S(1)}, bf16[256,256]{1,0:T(8,128)(2,1)S(1)}, u32[]{:S(2)}, u32[]{:S(2)}) collective-permute-start(bf16[256,256]{1,0:T(8,128)(2,1)S(1)} %collective-permute-done.2), channel_id=1, source_target_pairs={{0,2},{2,4},{4,6},{6,8},{8,10},{10,12},{12,14},{14,0},{1,3},{3,5},... | collective-permute-start | bytes 393224 | tf_op jit(solution)/shard_map/ppermute | solution.py:51
  126.2 8.7 %collective-permute-start.4 = (bf16[256,256]{1,0:T(8,128)(2,1)S(1)}, bf16[256,256]{1,0:T(8,128)(2,1)S(1)}, u32[]{:S(2)}, u32[]{:S(2)}) collective-permute-start(bf16[256,256]{1,0:T(8,128)(2,1)S(1)} %collective-permute-done.3), channel_id=1, source_target_pairs={{0,2},{2,4},{4,6},{6,8},{8,10},{10,12},{12,14},{14,0},{1,3},{3,5},... | collective-permute-start | bytes 393224 | tf_op jit(solution)/shard_map/ppermute | solution.py:51
  134.9 8.3 %collective-permute-start.5 = (bf16[256,256]{1,0:T(8,128)(2,1)S(1)}, bf16[256,256]{1,0:T(8,128)(2,1)S(1)}, u32[]{:S(2)}, u32[]{:S(2)}) collective-permute-start(bf16[256,256]{1,0:T(8,128)(2,1)S(1)} %collective-permute-done.4), channel_id=1, source_target_pairs={{0,2},{2,4},{4,6},{6,8},{8,10},{10,12},{12,14},{14,0},{1,3},{3,5},... | collective-permute-start | bytes 393224 | tf_op jit(solution)/shard_map/ppermute | solution.py:51
  143.2 7.7 %collective-permute-start.6 = (bf16[256,256]{1,0:T(8,128)(2,1)S(1)}, bf16[256,256]{1,0:T(8,128)(2,1)S(1)}, u32[]{:S(2)}, u32[]{:S(2)}) collective-permute-start(bf16[256,256]{1,0:T(8,128)(2,1)S(1)} %collective-permute-done.5), channel_id=1, source_target_pairs={{0,2},{2,4},{4,6},{6,8},{8,10},{10,12},{12,14},{14,0},{1,3},{3,5},... | collective-permute-start | bytes 393224 | tf_op jit(solution)/shard_map/ppermute | solution.py:51
  150.9 7.7 %collective-permute-start.7 = (bf16[256,256]{1,0:T(8,128)(2,1)S(1)}, bf16[256,256]{1,0:T(8,128)(2,1)S(1)}, u32[]{:S(2)}, u32[]{:S(2)}) collective-permute-start(bf16[256,256]{1,0:T(8,128)(2,1)S(1)} %collective-permute-done.6), channel_id=1, source_target_pairs={{0,2},{2,4},{4,6},{6,8},{8,10},{10,12},{12,14},{14,0},{1,3},{3,5},... | collective-permute-start | bytes 393224 | tf_op jit(solution)/shard_map/ppermute | solution.py:51
  161.5 84.8 %reduce-scatter.7.cloned.1.call-start = ((), (), s32[]{:S(2)}) async-start(), calls=%async_computation.8 | async-start | bytes 1179648 | tf_op jit(solution)/shard_map/reduce_scatter | solution.py:46
  181.0 140.5 %all-reduce.7.cloned.1.call-start = ((), (), s32[]{:S(2)}) async-start(), calls=%async_computation.9 | async-start | bytes 524288 | tf_op jit(solution)/shard_map/psum | solution.py:55
  246.3 56.7 %copy-start.4 = (bf16[256,256]{1,0:T(8,128)(2,1)S(1)}, bf16[256,256]{1,0:T(8,128)(2,1)}, u32[]{:S(2)}) copy-start(bf16[256,256]{1,0:T(8,128)(2,1)} %reduce-scatter.7.cloned.1.call-done) | copy-start | bytes 393220
  247.5 7.7 %collective-permute-start.8 = (bf16[256,256]{1,0:T(8,128)(2,1)S(1)}, bf16[256,256]{1,0:T(8,128)(2,1)S(1)}, u32[]{:S(2)}, u32[]{:S(2)}) collective-permute-start(bf16[256,256]{1,0:T(8,128)(2,1)S(1)} %fusion.55), channel_id=1, source_target_pairs={{0,2},{2,4},{4,6},{6,8},{8,10},{10,12},{12,14},{14,0},{1,3},{3,5},... | collective-permute-start | bytes 393224 | tf_op jit(solution)/shard_map/ppermute | solution.py:51
  255.2 7.7 %collective-permute-start.9 = (bf16[256,256]{1,0:T(8,128)(2,1)S(1)}, bf16[256,256]{1,0:T(8,128)(2,1)S(1)}, u32[]{:S(2)}, u32[]{:S(2)}) collective-permute-start(bf16[256,256]{1,0:T(8,128)(2,1)S(1)} %collective-permute-done.8), channel_id=1, source_target_pairs={{0,2},{2,4},{4,6},{6,8},{8,10},{10,12},{12,14},{14,0},{1,3},{3,5},... | collective-permute-start | bytes 393224 | tf_op jit(solution)/shard_map/ppermute | solution.py:51
  262.8 7.7 %collective-permute-start.10 = (bf16[256,256]{1,0:T(8,128)(2,1)S(1)}, bf16[256,256]{1,0:T(8,128)(2,1)S(1)}, u32[]{:S(2)}, u32[]{:S(2)}) collective-permute-start(bf16[256,256]{1,0:T(8,128)(2,1)S(1)} %collective-permute-done.9), channel_id=1, source_target_pairs={{0,2},{2,4},{4,6},{6,8},{8,10},{10,12},{12,14},{14,0},{1,3},{3,5},... | collective-permute-start | bytes 393224 | tf_op jit(solution)/shard_map/ppermute | solution.py:51
  270.5 8.8 %collective-permute-start.11 = (bf16[256,256]{1,0:T(8,128)(2,1)S(1)}, bf16[256,256]{1,0:T(8,128)(2,1)S(1)}, u32[]{:S(2)}, u32[]{:S(2)}) collective-permute-start(bf16[256,256]{1,0:T(8,128)(2,1)S(1)} %collective-permute-done.10), channel_id=1, source_target_pairs={{0,2},{2,4},{4,6},{6,8},{8,10},{10,12},{12,14},{14,0},{1,3},{3,5},... | collective-permute-start | bytes 393224 | tf_op jit(solution)/shard_map/ppermute | solution.py:51
  279.3 8.2 %collective-permute-start.12 = (bf16[256,256]{1,0:T(8,128)(2,1)S(1)}, bf16[256,256]{1,0:T(8,128)(2,1)S(1)}, u32[]{:S(2)}, u32[]{:S(2)}) collective-permute-start(bf16[256,256]{1,0:T(8,128)(2,1)S(1)} %collective-permute-done.11), channel_id=1, source_target_pairs={{0,2},{2,4},{4,6},{6,8},{8,10},{10,12},{12,14},{14,0},{1,3},{3,5},... | collective-permute-start | bytes 393224 | tf_op jit(solution)/shard_map/ppermute | solution.py:51
  287.5 7.7 %collective-permute-start.13 = (bf16[256,256]{1,0:T(8,128)(2,1)S(1)}, bf16[256,256]{1,0:T(8,128)(2,1)S(1)}, u32[]{:S(2)}, u32[]{:S(2)}) collective-permute-start(bf16[256,256]{1,0:T(8,128)(2,1)S(1)} %collective-permute-done.12), channel_id=1, source_target_pairs={{0,2},{2,4},{4,6},{6,8},{8,10},{10,12},{12,14},{14,0},{1,3},{3,5},... | collective-permute-start | bytes 393224 | tf_op jit(solution)/shard_map/ppermute | solution.py:51
  295.2 7.7 %collective-permute-start.14 = (bf16[256,256]{1,0:T(8,128)(2,1)S(1)}, bf16[256,256]{1,0:T(8,128)(2,1)S(1)}, u32[]{:S(2)}, u32[]{:S(2)}) collective-permute-start(bf16[256,256]{1,0:T(8,128)(2,1)S(1)} %collective-permute-done.13), channel_id=1, source_target_pairs={{0,2},{2,4},{4,6},{6,8},{8,10},{10,12},{12,14},{14,0},{1,3},{3,5},... | collective-permute-start | bytes 393224 | tf_op jit(solution)/shard_map/ppermute | solution.py:51
  305.8 84.6 %reduce-scatter.9.cloned.1.call-start = ((), (), s32[]{:S(2)}) async-start(), calls=%async_computation.10 | async-start | bytes 1179648 | tf_op jit(solution)/shard_map/reduce_scatter | solution.py:46
  325.2 140.4 %all-reduce.9.cloned.1.call-start = ((), (), s32[]{:S(2)}) async-start(), calls=%async_computation.11 | async-start | bytes 524288 | tf_op jit(solution)/shard_map/psum | solution.py:55
  390.5 56.7 %copy-start.5 = (bf16[256,256]{1,0:T(8,128)(2,1)S(1)}, bf16[256,256]{1,0:T(8,128)(2,1)}, u32[]{:S(2)}) copy-start(bf16[256,256]{1,0:T(8,128)(2,1)} %reduce-scatter.9.cloned.1.call-done) | copy-start | bytes 393220
  391.6 7.7 %collective-permute-start.15 = (bf16[256,256]{1,0:T(8,128)(2,1)S(1)}, bf16[256,256]{1,0:T(8,128)(2,1)S(1)}, u32[]{:S(2)}, u32[]{:S(2)}) collective-permute-start(bf16[256,256]{1,0:T(8,128)(2,1)S(1)} %fusion.63), channel_id=1, source_target_pairs={{0,2},{2,4},{4,6},{6,8},{8,10},{10,12},{12,14},{14,0},{1,3},{3,5},... | collective-permute-start | bytes 393224 | tf_op jit(solution)/shard_map/ppermute | solution.py:51
  399.3 7.7 %collective-permute-start.16 = (bf16[256,256]{1,0:T(8,128)(2,1)S(1)}, bf16[256,256]{1,0:T(8,128)(2,1)S(1)}, u32[]{:S(2)}, u32[]{:S(2)}) collective-permute-start(bf16[256,256]{1,0:T(8,128)(2,1)S(1)} %collective-permute-done.15), channel_id=1, source_target_pairs={{0,2},{2,4},{4,6},{6,8},{8,10},{10,12},{12,14},{14,0},{1,3},{3,5},... | collective-permute-start | bytes 393224 | tf_op jit(solution)/shard_map/ppermute | solution.py:51
  407.0 7.7 %collective-permute-start.17 = (bf16[256,256]{1,0:T(8,128)(2,1)S(1)}, bf16[256,256]{1,0:T(8,128)(2,1)S(1)}, u32[]{:S(2)}, u32[]{:S(2)}) collective-permute-start(bf16[256,256]{1,0:T(8,128)(2,1)S(1)} %collective-permute-done.16), channel_id=1, source_target_pairs={{0,2},{2,4},{4,6},{6,8},{8,10},{10,12},{12,14},{14,0},{1,3},{3,5},... | collective-permute-start | bytes 393224 | tf_op jit(solution)/shard_map/ppermute | solution.py:51
  414.7 8.8 %collective-permute-start.18 = (bf16[256,256]{1,0:T(8,128)(2,1)S(1)}, bf16[256,256]{1,0:T(8,128)(2,1)S(1)}, u32[]{:S(2)}, u32[]{:S(2)}) collective-permute-start(bf16[256,256]{1,0:T(8,128)(2,1)S(1)} %collective-permute-done.17), channel_id=1, source_target_pairs={{0,2},{2,4},{4,6},{6,8},{8,10},{10,12},{12,14},{14,0},{1,3},{3,5},... | collective-permute-start | bytes 393224 | tf_op jit(solution)/shard_map/ppermute | solution.py:51
  423.4 8.2 %collective-permute-start.19 = (bf16[256,256]{1,0:T(8,128)(2,1)S(1)}, bf16[256,256]{1,0:T(8,128)(2,1)S(1)}, u32[]{:S(2)}, u32[]{:S(2)}) collective-permute-start(bf16[256,256]{1,0:T(8,128)(2,1)S(1)} %collective-permute-done.18), channel_id=1, source_target_pairs={{0,2},{2,4},{4,6},{6,8},{8,10},{10,12},{12,14},{14,0},{1,3},{3,5},... | collective-permute-start | bytes 393224 | tf_op jit(solution)/shard_map/ppermute | solution.py:51
  431.7 7.7 %collective-permute-start.20 = (bf16[256,256]{1,0:T(8,128)(2,1)S(1)}, bf16[256,256]{1,0:T(8,128)(2,1)S(1)}, u32[]{:S(2)}, u32[]{:S(2)}) collective-permute-start(bf16[256,256]{1,0:T(8,128)(2,1)S(1)} %collective-permute-done.19), channel_id=1, source_target_pairs={{0,2},{2,4},{4,6},{6,8},{8,10},{10,12},{12,14},{14,0},{1,3},{3,5},... | collective-permute-start | bytes 393224 | tf_op jit(solution)/shard_map/ppermute | solution.py:51
  439.3 7.7 %collective-permute-start.21 = (bf16[256,256]{1,0:T(8,128)(2,1)S(1)}, bf16[256,256]{1,0:T(8,128)(2,1)S(1)}, u32[]{:S(2)}, u32[]{:S(2)}) collective-permute-start(bf16[256,256]{1,0:T(8,128)(2,1)S(1)} %collective-permute-done.20), channel_id=1, source_target_pairs={{0,2},{2,4},{4,6},{6,8},{8,10},{10,12},{12,14},{14,0},{1,3},{3,5},... | collective-permute-start | bytes 393224 | tf_op jit(solution)/shard_map/ppermute | solution.py:51
  450.0 84.7 %reduce-scatter.11.cloned.1.call-start = ((), (), s32[]{:S(2)}) async-start(), calls=%async_computation.12 | async-start | bytes 1179648 | tf_op jit(solution)/shard_map/reduce_scatter | solution.py:46
  469.4 140.5 %all-reduce.11.cloned.1.call-start = ((), (), s32[]{:S(2)}) async-start(), calls=%async_computation.13 | async-start | bytes 524288 | tf_op jit(solution)/shard_map/psum | solution.py:55
  534.7 56.7 %copy-start.6 = (bf16[256,256]{1,0:T(8,128)(2,1)S(1)}, bf16[256,256]{1,0:T(8,128)(2,1)}, u32[]{:S(2)}) copy-start(bf16[256,256]{1,0:T(8,128)(2,1)} %reduce-scatter.11.cloned.1.call-done) | copy-start | bytes 393220
  535.9 7.7 %collective-permute-start.22 = (bf16[256,256]{1,0:T(8,128)(2,1)S(1)}, bf16[256,256]{1,0:T(8,128)(2,1)S(1)}, u32[]{:S(2)}, u32[]{:S(2)}) collective-permute-start(bf16[256,256]{1,0:T(8,128)(2,1)S(1)} %fusion.71), channel_id=1, source_target_pairs={{0,2},{2,4},{4,6},{6,8},{8,10},{10,12},{12,14},{14,0},{1,3},{3,5},... | collective-permute-start | bytes 393224 | tf_op jit(solution)/shard_map/ppermute | solution.py:51
  543.6 7.7 %collective-permute-start.23 = (bf16[256,256]{1,0:T(8,128)(2,1)S(1)}, bf16[256,256]{1,0:T(8,128)(2,1)S(1)}, u32[]{:S(2)}, u32[]{:S(2)}) collective-permute-start(bf16[256,256]{1,0:T(8,128)(2,1)S(1)} %collective-permute-done.22), channel_id=1, source_target_pairs={{0,2},{2,4},{4,6},{6,8},{8,10},{10,12},{12,14},{14,0},{1,3},{3,5},... | collective-permute-start | bytes 393224 | tf_op jit(solution)/shard_map/ppermute | solution.py:51
  551.2 7.7 %collective-permute-start.24 = (bf16[256,256]{1,0:T(8,128)(2,1)S(1)}, bf16[256,256]{1,0:T(8,128)(2,1)S(1)}, u32[]{:S(2)}, u32[]{:S(2)}) collective-permute-start(bf16[256,256]{1,0:T(8,128)(2,1)S(1)} %collective-permute-done.23), channel_id=1, source_target_pairs={{0,2},{2,4},{4,6},{6,8},{8,10},{10,12},{12,14},{14,0},{1,3},{3,5},... | collective-permute-start | bytes 393224 | tf_op jit(solution)/shard_map/ppermute | solution.py:51
  558.9 8.8 %collective-permute-start.25 = (bf16[256,256]{1,0:T(8,128)(2,1)S(1)}, bf16[256,256]{1,0:T(8,128)(2,1)S(1)}, u32[]{:S(2)}, u32[]{:S(2)}) collective-permute-start(bf16[256,256]{1,0:T(8,128)(2,1)S(1)} %collective-permute-done.24), channel_id=1, source_target_pairs={{0,2},{2,4},{4,6},{6,8},{8,10},{10,12},{12,14},{14,0},{1,3},{3,5},... | collective-permute-start | bytes 393224 | tf_op jit(solution)/shard_map/ppermute | solution.py:51
  567.7 8.2 %collective-permute-start.26 = (bf16[256,256]{1,0:T(8,128)(2,1)S(1)}, bf16[256,256]{1,0:T(8,128)(2,1)S(1)}, u32[]{:S(2)}, u32[]{:S(2)}) collective-permute-start(bf16[256,256]{1,0:T(8,128)(2,1)S(1)} %collective-permute-done.25), channel_id=1, source_target_pairs={{0,2},{2,4},{4,6},{6,8},{8,10},{10,12},{12,14},{14,0},{1,3},{3,5},... | collective-permute-start | bytes 393224 | tf_op jit(solution)/shard_map/ppermute | solution.py:51
  575.9 7.7 %collective-permute-start.27 = (bf16[256,256]{1,0:T(8,128)(2,1)S(1)}, bf16[256,256]{1,0:T(8,128)(2,1)S(1)}, u32[]{:S(2)}, u32[]{:S(2)}) collective-permute-start(bf16[256,256]{1,0:T(8,128)(2,1)S(1)} %collective-permute-done.26), channel_id=1, source_target_pairs={{0,2},{2,4},{4,6},{6,8},{8,10},{10,12},{12,14},{14,0},{1,3},{3,5},... | collective-permute-start | bytes 393224 | tf_op jit(solution)/shard_map/ppermute | solution.py:51
  583.6 7.7 %collective-permute-start.28 = (bf16[256,256]{1,0:T(8,128)(2,1)S(1)}, bf16[256,256]{1,0:T(8,128)(2,1)S(1)}, u32[]{:S(2)}, u32[]{:S(2)}) collective-permute-start(bf16[256,256]{1,0:T(8,128)(2,1)S(1)} %collective-permute-done.27), channel_id=1, source_target_pairs={{0,2},{2,4},{4,6},{6,8},{8,10},{10,12},{12,14},{14,0},{1,3},{3,5},... | collective-permute-start | bytes 393224 | tf_op jit(solution)/shard_map/ppermute | solution.py:51
  611.5 13.2 %all-to-all-start.1 = ((bf16[8,32,256]{2,1,0:T(8,128)(2,1)}), bf16[8,32,256]{2,1,0:T(8,128)(2,1)S(1)}, u32[]{:S(2)}, u32[]{:S(2)}) async-start(bf16[8,32,256]{2,1,0:T(8,128)(2,1)} %bitcast.27), calls=%async_computation.5 | async-start | bytes 262144 | tf_op jit(solution)/shard_map/all_to_all | solution.py:83
Sparse Core Ops, SparseCore 0:
  40.1 61.8 reduce-scatter.4
  161.7 15.5 all-reduce.4
  181.1 65.1 reduce-scatter.6
  305.9 15.4 all-reduce.6
  325.3 65.0 reduce-scatter.8
  450.1 15.4 all-reduce.8
  469.5 65.1 reduce-scatter.10
  594.3 15.4 all-reduce.10
